TPU v7x, 256 devices: a whole 4x4x8 slice. The times are simulated.
256 devices in a mesh: head: 4 (over x_hi, core), vis: 32 (over y, z), sec: 2 (over x_lo).
Axes of the slice: x: 4 (x_hi: 2, x_lo: 2; x = x_hi * 2 + x_lo), y: 4, z: 8, core: 2. Of those that a mesh axis runs over, the one named last changes fastest.
Arguments:
- text_states: bfloat16 [256, 8192], P(None, 'vis'), may hold values from -6 to 6
- w_query: bfloat16 [8192, 8192], P('vis', ('head', 'sec')), may hold values from -0.0625 to 0.0625
- w_out: bfloat16 [8192, 8192], P(('head', 'sec'), 'vis'), may hold values from -0.25 to 0.25
- visual_keys: bfloat16 [262144, 1024], P('vis', ('head', 'sec')), may hold values from -120 to 120
- visual_values: bfloat16 [262144, 1024], P('vis', ('head', 'sec')), may hold values from -6 to 6
- block_list: int32 [2, 32, 32], P(None, 'vis'), may hold values from -1 to 63, as said below
Outputs:
- projected: bfloat16 [256, 8192], P(('head', 'sec'), 'vis')
Inputs may be any that keep to these rules, and one draw needn't show every extreme that they name: `block_list`: for each query block and shard, the entries that are not -1 are distinct and come first; each query block selects exactly 512 key blocks in all (a quarter), between 0 and 32 from one shard, and exactly 32 from some shard.
All inputs are finite; a program needn't handle non-finite values.
Results may differ from a plain program's by a relative error of at most 0.012.
Values may be sent and summed in bfloat16 or wider, within the bound.
No kernel may reach another device: no remote copies, remote signals or barrier semaphores. Data moves between devices by JAX's collectives and lax.ppermute only.
A program may use at most 192 MiB of HBM per device.

v0:
```python
import jax
import jax.numpy as jnp
from jax import lax
from jax.sharding import PartitionSpec as P

QUERY_HEADS = 64
KEY_VALUE_HEADS = 8
HEAD_SIZE = 128
BLOCK_TOKENS = 128
NEG_FILL = -1e30


def combined_all(value, axis, join):
    pieces = jax.tree.map(lambda part: lax.all_gather(part, axis), value)
    head = jax.tree.map(lambda part: part[0], pieces)
    tail = jax.tree.map(lambda part: part[1:], pieces)
    subtotal, _ = lax.scan(lambda subtotal, piece: (join(subtotal, piece), None), head, tail)
    return subtotal


def block_partial(query_block, block_ids, blocked_keys, blocked_values):
    present = block_ids >= 0
    chosen = jnp.maximum(block_ids, 0)
    key_rows = blocked_keys[chosen]
    value_rows = blocked_values[chosen]
    scores = jnp.einsum(
        "tgqd,mbgd->tgqmb", query_block, key_rows, preferred_element_type=jnp.float32
    ) * HEAD_SIZE ** (-0.5)
    keep_mask = present[None, None, None, :, None]
    scores = jnp.where(keep_mask, scores, NEG_FILL)
    top_score = jnp.max(scores, axis=(3, 4))
    raised = jnp.where(keep_mask, jnp.exp(scores - top_score[:, :, :, None, None]), 0.0)
    denom_sum = jnp.sum(raised, axis=(3, 4))
    weighted = jnp.einsum(
        "tgqmb,mbgd->tgqd",
        raised.astype(jnp.bfloat16),
        value_rows,
        preferred_element_type=jnp.float32,
    )
    return (top_score, denom_sum, weighted)


def merge_pair(first, second):
    top_first, sum_first, acc_first = first
    top_second, sum_second, acc_second = second
    top_new = jnp.maximum(top_first, top_second)
    scale_first = jnp.exp(top_first - top_new)
    scale_second = jnp.exp(top_second - top_new)
    sum_new = sum_first * scale_first + sum_second * scale_second
    acc_new = acc_first * scale_first[:, :, None] + acc_second * scale_second[:, :, None]
    return (top_new, sum_new, acc_new)


def on_device(text_states, w_query, w_out, visual_keys, visual_values, block_list):
    tok_count = text_states.shape[0]
    group_count = visual_keys.shape[1] // HEAD_SIZE
    queries_per_group = QUERY_HEADS // KEY_VALUE_HEADS
    head_cols = group_count * queries_per_group
    local_terms = jnp.dot(text_states, w_query, preferred_element_type=jnp.float32)
    query_matrix = lax.psum(local_terms, "vis").astype(jnp.bfloat16)
    block_count = tok_count // BLOCK_TOKENS
    blocked_queries = query_matrix.reshape(
        block_count, BLOCK_TOKENS, group_count, queries_per_group, HEAD_SIZE
    )
    blocked_keys = visual_keys.reshape(-1, BLOCK_TOKENS, group_count, HEAD_SIZE)
    blocked_values = visual_values.reshape(-1, BLOCK_TOKENS, group_count, HEAD_SIZE)
    id_rows = block_list[:, 0, :]

    def per_block(packed):
        return block_partial(packed[0], packed[1], blocked_keys, blocked_values)

    top_score, denom_sum, weighted = lax.map(per_block, (blocked_queries, id_rows))
    top_score = top_score.reshape(tok_count, head_cols)
    denom_sum = denom_sum.reshape(tok_count, head_cols)
    weighted = weighted.reshape(tok_count, head_cols, HEAD_SIZE)
    merged_top, sum_all, acc_all = combined_all((top_score, denom_sum, weighted), "vis", merge_pair)
    attended = (
        (acc_all / sum_all[:, :, None])
        .reshape(tok_count, head_cols * HEAD_SIZE)
        .astype(jnp.bfloat16)
    )
    projected = lax.psum_scatter(
        jnp.dot(attended, w_out, preferred_element_type=jnp.float32),
        ("head", "sec"),
        scatter_dimension=0,
        tiled=True,
    )
    return projected.astype(jnp.bfloat16)


def solution(mesh):
    in_specs = (
        P(None, "vis"),
        P("vis", ("head", "sec")),
        P(("head", "sec"), "vis"),
        P("vis", ("head", "sec")),
        P("vis", ("head", "sec")),
        P(None, "vis", None),
    )
    out_specs = P(("head", "sec"), "vis")
    return jax.shard_map(
        on_device, mesh=mesh, in_specs=in_specs, out_specs=out_specs, check_vma=False
    )
```

profile of v0, /device:TPU:1, one launch (start us, length us, event | category | flops | bytes accessed | tf_op | source)
XLA Modules:
  0.0 589.2 jit_solution(97102992759839472)
XLA Ops:
  8.8 131.1 %all-reduce.1 = bf16[256,1024]{1,0:T(8,128)(2,1)S(1)} all-reduce(f32[256,1024]{1,0:T(8,128)S(1)} %fusion.25), channel_id=1, replica_groups=mesh['head'=4,'vis'=32,'sec'=2] {'vis'}, use_global_device_ids=true, to_apply=%region_0.0 | all-reduce | flops 262144 | bytes 1572864 | tf_op jit(solution)/shard_map/psum | solution.py:60
  140.0 60.2 %while.28 = (s32[]{:T(128)}, f32[2,128,1,8]{1,3,2,0:T(8,128)S(1)}, f32[2,128,1,8]{1,3,2,0:T(8,128)S(1)}, f32[2,128,1,8,128]{4,3,1,0,2:T(8,128)}, s32[2,32]{1,0:T...) while((s32[]{:T(128)}, f32[2,128,1,8]{1,3,2,0:T(8,128)S(1)}, ...), condition=%wide.region_4.5_spmd, body=%wide.region_1.4_spmd.sunk | while | flops 2202008576 | bytes 60069356 | solution.py:72
  140.7 2.3 gather_fusion
  143.7 7.0 %bitcast_reduce_fusion.2 = (f32[128,8]{0,1:T(8,128)S(1)}, f32[32,128,128,8]{2,1,3,0:T(8,128)}) fusion(pred[32]{0:T(512)(128)(4,1)S(1)} %compare_bitcast_fusion.2, bf16[1,128,1,8,128]{4,3,1,0,2:T(8,128)(2,1)S(1)} %constant_dynamic-slice_fusion.3, bf16[32,128,128]{2,1,0:T(8,128)(2,1)S(1)} %gather_fusion), kind=kOutput, calls=%fused_computation.11.clone.1 | convolution fusion | flops 1086323712 | bytes 18092064 | tf_op jit(solution)/shard_map/while/body/eval_jaxpr/tgqd,mbgd->tgqmb/dot_general | solution.py:26
  150.7 2.3 gather_fusion.1
  153.1 7.9 %fusion.38 = f32[1,128,1,8,128]{1,4,3,2,0:T(8,128)S(1)} fusion(f32[32,128,128,8]{2,1,3,0:T(8,128)} %get-tuple-element.247, f32[128,8]{0,1:T(8,128)S(1)} %get-tuple-element.248, pred[32]{0:T(512)(128)(4,1)S(1)} %compare_bitcast_fusion.2, bf16[32,128,128]{2,1,0:T(8,128)(2,1)S(1)} %gather_fusion.1), kind=kOutput, calls=%fused_computation.21.clone.1 | convolution fusion | flops 1094713344 | bytes 18354208 | tf_op jit(solution)/shard_map/while/body/eval_jaxpr/tgqmb,mbgd->tgqd/dot_general | solution.py:34
  162.0 8.0 %fusion.37 = f32[128,8]{0,1:T(8,128)S(1)} fusion(f32[32,128,128,8]{2,1,3,0:T(8,128)} %get-tuple-element.247, f32[128,8]{0,1:T(8,128)S(1)} %get-tuple-element.248, pred[32]{0:T(512)(128)(4,1)S(1)} %compare_bitcast_fusion.2), kind=kLoop, calls=%fused_computation.16.clone.1 | loop fusion | flops 20970496 | bytes 16785440 | tf_op jit(solution)/shard_map/while/body/eval_jaxpr/reduce_sum | solution.py:33
  170.8 2.3 gather_fusion
  173.8 7.0 %bitcast_reduce_fusion.2 = (f32[128,8]{0,1:T(8,128)S(1)}, f32[32,128,128,8]{2,1,3,0:T(8,128)}) fusion(pred[32]{0:T(512)(128)(4,1)S(1)} %compare_bitcast_fusion.2, bf16[1,128,1,8,128]{4,3,1,0,2:T(8,128)(2,1)S(1)} %constant_dynamic-slice_fusion.3, bf16[32,128,128]{2,1,0:T(8,128)(2,1)S(1)} %gather_fusion), kind=kOutput, calls=%fused_computation.11.clone.1 | convolution fusion | flops 1086323712 | bytes 18092064 | tf_op jit(solution)/shard_map/while/body/eval_jaxpr/tgqd,mbgd->tgqmb/dot_general | solution.py:26
  180.8 2.3 gather_fusion.1
  183.2 7.9 %fusion.38 = f32[1,128,1,8,128]{1,4,3,2,0:T(8,128)S(1)} fusion(f32[32,128,128,8]{2,1,3,0:T(8,128)} %get-tuple-element.247, f32[128,8]{0,1:T(8,128)S(1)} %get-tuple-element.248, pred[32]{0:T(512)(128)(4,1)S(1)} %compare_bitcast_fusion.2, bf16[32,128,128]{2,1,0:T(8,128)(2,1)S(1)} %gather_fusion.1), kind=kOutput, calls=%fused_computation.21.clone.1 | convolution fusion | flops 1094713344 | bytes 18354208 | tf_op jit(solution)/shard_map/while/body/eval_jaxpr/tgqmb,mbgd->tgqd/dot_general | solution.py:34
  192.1 8.0 %fusion.37 = f32[128,8]{0,1:T(8,128)S(1)} fusion(f32[32,128,128,8]{2,1,3,0:T(8,128)} %get-tuple-element.247, f32[128,8]{0,1:T(8,128)S(1)} %get-tuple-element.248, pred[32]{0:T(512)(128)(4,1)S(1)} %compare_bitcast_fusion.2), kind=kLoop, calls=%fused_computation.16.clone.1 | loop fusion | flops 20970496 | bytes 16785440 | tf_op jit(solution)/shard_map/while/body/eval_jaxpr/reduce_sum | solution.py:33
  200.2 34.1 %all_gather.9 = f32[32,256,8]{1,2,0:T(8,128)S(1)} all-gather(f32[1,256,8]{1,2,0:T(8,128)S(1)} %bitcast.159), channel_id=1, replica_groups=mesh['head'=4,'vis'=32,'sec'=2] {'vis'}, dimensions={0}, use_global_device_ids=true | all-gather | bytes 270336 | tf_op jit(solution)/shard_map/all_gather | solution.py:14
  234.3 43.5 %all_gather.10 = f32[32,256,8]{1,2,0:T(8,128)S(1)} all-gather(f32[1,256,8]{1,2,0:T(8,128)S(1)} %bitcast.160), channel_id=1, replica_groups=mesh['head'=4,'vis'=32,'sec'=2] {'vis'}, dimensions={0}, use_global_device_ids=true | all-gather | bytes 270336 | tf_op jit(solution)/shard_map/all_gather | solution.py:14
  277.9 178.2 %all-gather.2.cloned.1.call-done = f32[32,256,8,128]{3,2,1,0:T(8,128)} async-done(((f32[1,256,8,128]{3,2,1,0:T(8,128)}), f32[32,256,8,128]{3,2,1,0:T(8,128)}) %all-gather.2.cloned.1.call-update) | async-done | bytes 33554448 | tf_op jit(solution)/shard_map/all_gather | solution.py:14
  456.0 22.7 %slice.33 = f32[31,256,8,128]{3,2,1,0:T(8,128)} slice(f32[32,256,8,128]{3,2,1,0:T(8,128)} %all-gather.2.cloned.1.call-done), slice={[1:32], [0:256], [0:8], [0:128]} | slice | bytes 65011712 | tf_op jit(solution)/shard_map/slice | solution.py:16
  480.0 68.2 %while.29 = (s32[]{:T(128)}, f32[256,8]{0,1:T(8,128)S(1)}, f32[256,8]{0,1:T(8,128)S(1)}, f32[256,8,128]{2,1,0:T(8,128)S(1)}, f32[31,256,8]{1,2,0:T(8,128)S(1)}, ...) while((s32[]{:T(128)}, f32[256,8]{0,1:T(8,128)S(1)}, f32[256,8]{0,1:T(8,128)S(1)}, ...), condition=%wide.region_6.7_spmd, body=%wide.region_5.6_spmd.sunk | while | flops 798722 | bytes 3260509 | solution.py:17
  480.3 1.9 fusion.40
  482.5 1.9 fusion.40
  484.7 1.9 fusion.40
  486.9 1.9 fusion.40
  489.1 1.9 fusion.40
  491.3 1.9 fusion.40
  493.5 1.9 fusion.40
  495.7 1.9 fusion.40
  497.9 1.9 fusion.40
  500.2 1.9 fusion.40
  502.4 1.9 fusion.40
  504.6 1.9 fusion.40
  506.8 1.9 fusion.40
  509.0 1.9 fusion.40
  511.2 1.9 fusion.40
  513.4 1.9 fusion.40
  515.6 1.9 fusion.40
  517.8 1.9 fusion.40
  520.0 1.9 fusion.40
  522.2 1.9 fusion.40
  524.4 1.9 fusion.40
  526.6 1.9 fusion.40
  528.8 1.9 fusion.40
  533.2 1.9 fusion.40
  535.4 1.9 fusion.40
  537.6 1.9 fusion.40
  539.8 1.9 fusion.40
  542.0 1.9 fusion.40
  544.2 1.9 fusion.40
  546.4 1.9 fusion.40
  549.8 31.2 %reduce-scatter.2.cloned.1.call-done = f32[32,256]{1,0:T(8,128)} async-done(((f32[256,256]{1,0:T(8,128)}), f32[32,256]{1,0:T(8,128)}) %reduce-scatter.2.cloned.1.call-update) | async-done | bytes 32784 | tf_op jit(solution)/shard_map/reduce_scatter | solution.py:82
  (132 shorter events, 21.8 us)
Async XLA Ops:
  6.5 1.0 copy-start
  6.5 449.5 %all-gather.2.cloned.1.call-start = ((), (), s32[]{:S(2)}) async-start(), calls=%async_computation.1 | async-start | bytes 34603008 | tf_op jit(solution)/shard_map/all_gather | solution.py:14
  200.2 380.8 %reduce-scatter.2.cloned.1.call-start = ((), (), s32[]{:S(2)}) async-start(), calls=%async_computation.2 | async-start | bytes 294912 | tf_op jit(solution)/shard_map/reduce_scatter | solution.py:82
  456.0 126.4 %copy-start.1 = (bf16[256,1024]{1,0:T(8,128)(2,1)S(1)}, bf16[256,1024]{1,0:T(8,128)(2,1)}, u32[]{:S(2)}) copy-start(bf16[256,1024]{1,0:T(8,128)(2,1)} %param.11) | copy-start | bytes 1572868
  478.7 70.1 %copy-start.2 = (bf16[1024,256]{1,0:T(8,128)(2,1)S(1)}, bf16[1024,256]{1,0:T(8,128)(2,1)}, u32[]{:S(2)}) copy-start(bf16[1024,256]{1,0:T(8,128)(2,1)} %param.12) | copy-start | bytes 1572868
Sparse Core Ops, SparseCore 0:
  200.3 255.6 all-gather.1
  549.9 31.0 reduce-scatter.1
where the time goes:
time: 591 us; the launch traced here: 589 us
  blocking collectives  209 us (35%)
  waiting for transfers between devices  209 us (35%)
  other arithmetic  79.7 us (13%)
  local copies, waits for them, and re-layouts  44.6 us (8%)
  matrix products  31.9 us (5%)
  between operations  13.5 us (2%)
    all_gather x1, waiting for transfers between devices, combined_all(): pieces = jax.tree.map(lambda part: lax.all_gather(part, axis), value)  178 us
    psum x1, blocking collectives, on_device(): query_matrix = lax.psum(local_terms, 'vis').astype(jnp.bfloat16)  131 us
    all_gather x2, blocking collectives, combined_all(): pieces = jax.tree.map(lambda part: lax.all_gather(part, axis), value)  77.6 us
    add x31, other arithmetic, merge_pair(): acc_first * scale_first[:, :, None] + acc_second * scale_second[:, :, None]  58.7 us
    reduce_scatter x1, waiting for transfers between devices, on_device(): lax.psum_scatter(jnp.dot(attended, w_out, preferred_element_type=jnp.floa...  31.2 us
    slice x3, local copies, waits for them, and re-layouts, combined_all(): tail = jax.tree.map(lambda part: part[1:], pieces)  22.7 us
    reduce_sum x2, other arithmetic, block_partial(): denom_sum = jnp.sum(raised, axis=(3, 4))  16 us
    dot_general x2, matrix products, block_partial(): jnp.einsum('tgqmb,mbgd->tgqd', raised.astype(jnp.bfloat16), value_rows, p...  15.7 us
  transfers between devices with their start and end apart: 2, of which 2 were waited for; matrix products, arithmetic and copies ran while one was open for 0% of the time, Pallas kernels for 0%

commit v1 on v0

--- a/solution.py
+++ b/solution.py
@@ -57,7 +57,7 @@
     queries_per_group = QUERY_HEADS // KEY_VALUE_HEADS
     head_cols = group_count * queries_per_group
     local_terms = jnp.dot(text_states, w_query, preferred_element_type=jnp.float32)
-    query_matrix = lax.psum(local_terms, "vis").astype(jnp.bfloat16)
+    query_matrix = jnp.sum(lax.all_gather(local_terms, "vis"), axis=0).astype(jnp.bfloat16)
     block_count = tok_count // BLOCK_TOKENS
     blocked_queries = query_matrix.reshape(
         block_count, BLOCK_TOKENS, group_count, queries_per_group, HEAD_SIZE

time: 591 us -> 683 us (1.16)
  waiting for transfers between devices: 209 us -> 420 us
  blocking collectives: 209 us -> 79.3 us
  other arithmetic: 79.7 us -> 88.9 us
    all_gather x0 -> x1, waiting for transfers between devices: none -> 236 us  [on_device(): lax.all_gather(local_terms, 'vis')]
    psum x1 -> x0, blocking collectives: 131 us -> none  [on_device(): query_matrix = lax.psum(local_terms, 'vis').astype(jnp.bfloat16)]
    all_gather x1, waiting for transfers between devices: 178 us -> 153 us  [combined_all(): pieces = jax.tree.map(lambda part: lax.all_gather(part, axis), value)]
    reduce_sum x0 -> x1, other arithmetic: none -> 11.9 us  [on_device(): jnp.sum(lax.all_gather(local_terms, 'vis'), axis=0).astype(jnp.bfloat16)]
  transfers between devices with their start and end apart: 2 -> 3, of which waited for: 2 -> 3; matrix products, arithmetic and copies ran while one was open for 0% -> 0% of each run, Pallas kernels for 0% -> 0%
where the time goes in v1:
time: 683 us; the launch traced here: 681 us
  waiting for transfers between devices  420 us (61%)
  other arithmetic  88.9 us (13%)
  blocking collectives  79.3 us (12%)
  local copies, waits for them, and re-layouts  44.6 us (7%)
  matrix products  33 us (5%)
  between operations  13.2 us (2%)
    all_gather x1, waiting for transfers between devices, on_device(): lax.all_gather(local_terms, 'vis')  236 us
    all_gather x1, waiting for transfers between devices, combined_all(): pieces = jax.tree.map(lambda part: lax.all_gather(part, axis), value)  153 us
    all_gather x2, blocking collectives, combined_all(): pieces = jax.tree.map(lambda part: lax.all_gather(part, axis), value)  79.3 us
    add x31, other arithmetic, merge_pair(): acc_first * scale_first[:, :, None] + acc_second * scale_second[:, :, None]  58.7 us
    reduce_scatter x1, waiting for transfers between devices, on_device(): lax.psum_scatter(jnp.dot(attended, w_out, preferred_element_type=jnp.floa...  31.3 us
    slice x3, local copies, waits for them, and re-layouts, combined_all(): tail = jax.tree.map(lambda part: part[1:], pieces)  22.6 us
    reduce_sum x2, other arithmetic, block_partial(): denom_sum = jnp.sum(raised, axis=(3, 4))  16 us
    dot_general x2, matrix products, block_partial(): jnp.einsum('tgqmb,mbgd->tgqd', raised.astype(jnp.bfloat16), value_rows, p...  15.7 us
  transfers between devices with their start and end apart: 3, of which 3 were waited for; matrix products, arithmetic and copies ran while one was open for 0% of the time, Pallas kernels for 0%

profile of v1, /device:TPU:1, one launch (start us, length us, event | category | flops | bytes accessed | tf_op | source)
XLA Modules:
  0.0 680.9 jit_solution(11785829196143805052)
XLA Ops:
  7.6 2.2 fusion.25
  9.9 236.1 %all-gather.6.cloned.1.call-done = f32[8192,1024]{1,0:T(8,128)} async-done(((f32[256,1024]{1,0:T(8,128)}), f32[8192,1024]{1,0:T(8,128)}) %all-gather.6.cloned.1.call-update) | async-done | bytes 33554448 | tf_op jit(solution)/shard_map/all_gather | solution.py:60
  246.0 11.9 %reduce_sum.18 = bf16[256,1024]{1,0:T(8,128)(2,1)S(1)} reduce(f32[32,256,1024]{2,1,0:T(8,128)} %bitcast.152, f32[]{:T(128)} %constant.40.clone.1), dimensions={0}, to_apply=%region_0.0 | reduce | flops 8126464 | bytes 34078724 | tf_op jit(solution)/shard_map/reduce_sum | solution.py:60
  258.0 57.6 %while.28 = (s32[]{:T(128)}, f32[2,128,1,8]{1,3,2,0:T(8,128)S(1)}, f32[2,128,1,8]{1,3,2,0:T(8,128)S(1)}, f32[2,128,1,8,128]{4,3,1,0,2:T(8,128)}, s32[2,32]{1,0:T...) while((s32[]{:T(128)}, f32[2,128,1,8]{1,3,2,0:T(8,128)S(1)}, ...), condition=%wide.region_4.5_spmd, body=%wide.region_1.4_spmd.sunk | while | flops 2202008576 | bytes 60069356 | solution.py:72
  258.1 2.3 gather_fusion
  260.5 7.0 %bitcast_reduce_fusion.2 = (f32[128,8]{0,1:T(8,128)S(1)}, f32[32,128,128,8]{2,1,3,0:T(8,128)}) fusion(pred[32]{0:T(512)(128)(4,1)S(1)} %compare_bitcast_fusion.2, bf16[1,128,1,8,128]{4,3,1,0,2:T(8,128)(2,1)S(1)} %constant_dynamic-slice_fusion.3, bf16[32,128,128]{2,1,0:T(8,128)(2,1)S(1)} %gather_fusion), kind=kOutput, calls=%fused_computation.11.clone.1 | convolution fusion | flops 1086323712 | bytes 18092064 | tf_op jit(solution)/shard_map/while/body/eval_jaxpr/tgqd,mbgd->tgqmb/dot_general | solution.py:26
  267.5 2.3 gather_fusion.1
  269.8 7.9 %fusion.38 = f32[1,128,1,8,128]{1,4,3,2,0:T(8,128)S(1)} fusion(f32[32,128,128,8]{2,1,3,0:T(8,128)} %get-tuple-element.239, f32[128,8]{0,1:T(8,128)S(1)} %get-tuple-element.240, pred[32]{0:T(512)(128)(4,1)S(1)} %compare_bitcast_fusion.2, bf16[32,128,128]{2,1,0:T(8,128)(2,1)S(1)} %gather_fusion.1), kind=kOutput, calls=%fused_computation.21.clone.1 | convolution fusion | flops 1094713344 | bytes 18354208 | tf_op jit(solution)/shard_map/while/body/eval_jaxpr/tgqmb,mbgd->tgqd/dot_general | solution.py:34
  278.8 8.0 %fusion.37 = f32[128,8]{0,1:T(8,128)S(1)} fusion(f32[32,128,128,8]{2,1,3,0:T(8,128)} %get-tuple-element.239, f32[128,8]{0,1:T(8,128)S(1)} %get-tuple-element.240, pred[32]{0:T(512)(128)(4,1)S(1)} %compare_bitcast_fusion.2), kind=kLoop, calls=%fused_computation.16.clone.1 | loop fusion | flops 20970496 | bytes 16785440 | tf_op jit(solution)/shard_map/while/body/eval_jaxpr/reduce_sum | solution.py:33
  286.8 2.3 gather_fusion
  289.2 7.0 %bitcast_reduce_fusion.2 = (f32[128,8]{0,1:T(8,128)S(1)}, f32[32,128,128,8]{2,1,3,0:T(8,128)}) fusion(pred[32]{0:T(512)(128)(4,1)S(1)} %compare_bitcast_fusion.2, bf16[1,128,1,8,128]{4,3,1,0,2:T(8,128)(2,1)S(1)} %constant_dynamic-slice_fusion.3, bf16[32,128,128]{2,1,0:T(8,128)(2,1)S(1)} %gather_fusion), kind=kOutput, calls=%fused_computation.11.clone.1 | convolution fusion | flops 1086323712 | bytes 18092064 | tf_op jit(solution)/shard_map/while/body/eval_jaxpr/tgqd,mbgd->tgqmb/dot_general | solution.py:26
  296.2 2.3 gather_fusion.1
  298.6 7.9 %fusion.38 = f32[1,128,1,8,128]{1,4,3,2,0:T(8,128)S(1)} fusion(f32[32,128,128,8]{2,1,3,0:T(8,128)} %get-tuple-element.239, f32[128,8]{0,1:T(8,128)S(1)} %get-tuple-element.240, pred[32]{0:T(512)(128)(4,1)S(1)} %compare_bitcast_fusion.2, bf16[32,128,128]{2,1,0:T(8,128)(2,1)S(1)} %gather_fusion.1), kind=kOutput, calls=%fused_computation.21.clone.1 | convolution fusion | flops 1094713344 | bytes 18354208 | tf_op jit(solution)/shard_map/while/body/eval_jaxpr/tgqmb,mbgd->tgqd/dot_general | solution.py:34
  307.6 8.0 %fusion.37 = f32[128,8]{0,1:T(8,128)S(1)} fusion(f32[32,128,128,8]{2,1,3,0:T(8,128)} %get-tuple-element.239, f32[128,8]{0,1:T(8,128)S(1)} %get-tuple-element.240, pred[32]{0:T(512)(128)(4,1)S(1)} %compare_bitcast_fusion.2), kind=kLoop, calls=%fused_computation.16.clone.1 | loop fusion | flops 20970496 | bytes 16785440 | tf_op jit(solution)/shard_map/while/body/eval_jaxpr/reduce_sum | solution.py:33
  315.7 39.5 %all_gather.17 = f32[32,256,8]{1,2,0:T(8,128)S(1)} all-gather(f32[1,256,8]{1,2,0:T(8,128)S(1)} %bitcast.161), channel_id=1, replica_groups=mesh['head'=4,'vis'=32,'sec'=2] {'vis'}, dimensions={0}, use_global_device_ids=true | all-gather | bytes 270336 | tf_op jit(solution)/shard_map/all_gather | solution.py:14
  355.2 39.8 %all_gather.18 = f32[32,256,8]{1,2,0:T(8,128)S(1)} all-gather(f32[1,256,8]{1,2,0:T(8,128)S(1)} %bitcast.162), channel_id=1, replica_groups=mesh['head'=4,'vis'=32,'sec'=2] {'vis'}, dimensions={0}, use_global_device_ids=true | all-gather | bytes 270336 | tf_op jit(solution)/shard_map/all_gather | solution.py:14
  395.0 152.9 %all-gather.4.cloned.1.call-done = f32[32,256,8,128]{3,2,1,0:T(8,128)} async-done(((f32[1,256,8,128]{3,2,1,0:T(8,128)}), f32[32,256,8,128]{3,2,1,0:T(8,128)}) %all-gather.4.cloned.1.call-update) | async-done | bytes 33554448 | tf_op jit(solution)/shard_map/all_gather | solution.py:14
  547.9 22.6 %slice.33 = f32[31,256,8,128]{3,2,1,0:T(8,128)} slice(f32[32,256,8,128]{3,2,1,0:T(8,128)} %all-gather.4.cloned.1.call-done), slice={[1:32], [0:256], [0:8], [0:128]} | slice | bytes 65011712 | tf_op jit(solution)/shard_map/slice | solution.py:16
  571.9 68.2 %while.29 = (s32[]{:T(128)}, f32[256,8]{0,1:T(8,128)S(1)}, f32[256,8]{0,1:T(8,128)S(1)}, f32[256,8,128]{2,1,0:T(8,128)S(1)}, f32[31,256,8]{1,2,0:T(8,128)S(1)}, ...) while((s32[]{:T(128)}, f32[256,8]{0,1:T(8,128)S(1)}, f32[256,8]{0,1:T(8,128)S(1)}, ...), condition=%wide.region_6.7_spmd, body=%wide.region_5.6_spmd.sunk | while | flops 798722 | bytes 3260509 | solution.py:17
  572.2 1.9 fusion.40
  576.6 1.9 fusion.40
  578.8 1.9 fusion.40
  581.0 1.9 fusion.40
  583.2 1.9 fusion.40
  585.4 1.9 fusion.40
  587.6 1.9 fusion.40
  589.8 1.9 fusion.40
  592.0 1.9 fusion.40
  594.2 1.9 fusion.40
  596.4 1.9 fusion.40
  600.8 1.9 fusion.40
  603.0 1.9 fusion.40
  605.2 1.9 fusion.40
  607.4 1.9 fusion.40
  609.6 1.9 fusion.40
  611.8 1.9 fusion.40
  614.0 1.9 fusion.40
  618.4 1.9 fusion.40
  620.6 1.9 fusion.40
  622.8 1.9 fusion.40
  625.0 1.9 fusion.40
  627.2 1.9 fusion.40
  629.4 1.9 fusion.40
  631.6 1.9 fusion.40
  633.8 1.9 fusion.40
  636.0 1.9 fusion.40
  638.2 1.9 fusion.40
  641.7 31.3 %reduce-scatter.2.cloned.1.call-done = f32[32,256]{1,0:T(8,128)} async-done(((f32[256,256]{1,0:T(8,128)}), f32[32,256]{1,0:T(8,128)}) %reduce-scatter.2.cloned.1.call-update) | async-done | bytes 32784 | tf_op jit(solution)/shard_map/reduce_scatter | solution.py:82
  (137 shorter events, 21.8 us)
Async XLA Ops:
  6.5 1.0 copy-start
  6.5 239.5 %all-gather.6.cloned.1.call-start = ((), (), s32[]{:S(2)}) async-start(), calls=%async_computation.3 | async-start | bytes 34603008 | tf_op jit(solution)/shard_map/all_gather | solution.py:60
  9.8 538.1 %all-gather.4.cloned.1.call-start = ((), (), s32[]{:S(2)}) async-start(), calls=%async_computation.1 | async-start | bytes 34603008 | tf_op jit(solution)/shard_map/all_gather | solution.py:14
  246.0 12.0 %copy-start.3 = (s32[2,1,32]{2,1,0:T(1,128)S(1)}, s32[2,1,32]{2,1,0:T(1,128)}, u32[]{:S(2)}) copy-start(s32[2,1,32]{2,1,0:T(1,128)} %param.15) | copy-start | bytes 772
  315.6 357.4 %reduce-scatter.2.cloned.1.call-start = ((), (), s32[]{:S(2)}) async-start(), calls=%async_computation.2 | async-start | bytes 294912 | tf_op jit(solution)/shard_map/reduce_scatter | solution.py:82
  547.9 126.4 %copy-start.1 = (bf16[256,1024]{1,0:T(8,128)(2,1)S(1)}, bf16[256,1024]{1,0:T(8,128)(2,1)}, u32[]{:S(2)}) copy-start(bf16[256,1024]{1,0:T(8,128)(2,1)} %param.11) | copy-start | bytes 1572868
  570.5 70.1 %copy-start.2 = (bf16[1024,256]{1,0:T(8,128)(2,1)S(1)}, bf16[1024,256]{1,0:T(8,128)(2,1)}, u32[]{:S(2)}) copy-start(bf16[1024,256]{1,0:T(8,128)(2,1)} %param.12) | copy-start | bytes 1572868
Sparse Core Ops, SparseCore 0:
  10.0 235.9 all-gather.5
  315.7 232.1 all-gather.3
  641.8 31.1 reduce-scatter.1
